TPU v7x, 32 devices: a whole 2x2x4 slice. The times are simulated.
32 devices in a mesh: obs: 16 (over z, x, core), sp: 2 (over y).
Axes of the slice: x: 2, y: 2, z: 4, core: 2. Of those that a mesh axis runs over, the one named last changes fastest.
Arguments:
- descriptors: bfloat16 [16384, 512], P('obs'), may hold values from -10 to 10
- candidates: bfloat16 [8192, 512], P('obs'), may hold values from -10 to 10
- sparse_index: int32 [4096], replicated, may hold values from 0 to 8191, as said below
- targets: bfloat16 [16384], P('obs'), may hold values from -12 to 12
- regularizer: float32 [4096], replicated, may hold values from 0.25 to 1
Outputs:
- inverse: float32 [4096, 4096], P('sp', 'obs')
- weights: float32 [4096], P('sp')
Inputs may be any that keep to these rules, and one draw needn't show every extreme that they name: `sparse_index`: the 4096 indices are distinct.
All inputs are finite; a program needn't handle non-finite values.
Results may differ from a plain program's by a relative error of at most 0.012.
Values may be sent and summed in bfloat16 or wider, within the bound.
A program may use at most 128 MiB of HBM per device.

v0:
```python
import math
import jax
import jax.numpy as jnp
from jax import lax
from jax.sharding import PartitionSpec as P

epsilon = 1e-06


def unit_rows(row_block):
    values = row_block.astype(jnp.float32)
    return (values * lax.rsqrt(jnp.sum(values * values, axis=1, keepdims=True) + epsilon)).astype(
        jnp.bfloat16
    )


def kernel_block(normed, sparse):
    inner = lax.dot_general(
        normed, sparse, (((1,), (1,)), ((), ())), preferred_element_type=jnp.float32
    )
    scaled = inner * math.sqrt(normed.shape[1])
    squared = scaled * scaled
    return (squared * squared - 6.0 * squared + 3.0).astype(jnp.bfloat16)


def select_rows(candidate_units, wanted, cand_start):
    shifted = wanted - cand_start
    inside = (shifted >= 0) & (shifted < candidate_units.shape[0])
    picked = candidate_units[jnp.clip(shifted, 0, candidate_units.shape[0] - 1)].astype(jnp.float32)
    return picked * inside[:, None].astype(jnp.float32)


def first_iterate(system_part, row_scale, col_scale, on_diag):
    return (
        jnp.where(on_diag, 2.0 * row_scale[:, None], 0.0)
        - system_part * row_scale[:, None] * col_scale[None, :]
    )


def on_device(descriptors, candidates, sparse_index, targets, regularizer):
    obs_count = lax.axis_size("obs")
    sp_count = lax.axis_size("sp")
    obs_pos = lax.axis_index("obs")
    sp_pos = lax.axis_index("sp")
    sparse_count = sparse_index.shape[0]
    block_rows = sparse_count // sp_count
    tile_cols = sparse_count // obs_count
    rows_all = descriptors.shape[0] * obs_count
    normed = unit_rows(descriptors)
    candidate_units = unit_rows(candidates)
    cand_start = obs_pos * candidates.shape[0]
    all_sparse = lax.psum(
        select_rows(candidate_units, sparse_index, cand_start).astype(jnp.bfloat16), "obs"
    )
    full_kernel = kernel_block(normed, all_sparse)
    own_kernel = lax.dynamic_slice_in_dim(full_kernel, sp_pos * block_rows, block_rows, 1)
    gram_part = lax.psum_scatter(
        lax.dot_general(
            full_kernel, own_kernel, (((0,), (0,)), ((), ())), preferred_element_type=jnp.float32
        ),
        "obs",
        scatter_dimension=0,
        tiled=True,
    )
    weighted = jnp.dot(targets, own_kernel, preferred_element_type=jnp.float32)
    squares = jnp.sum(jnp.square(own_kernel.astype(jnp.float32)), axis=0)
    weighted, squares = lax.psum((weighted, squares), "obs")
    weighted, squares = (
        lax.all_gather(weighted, "sp", axis=0, tiled=True),
        lax.all_gather(squares, "sp", axis=0, tiled=True),
    )
    normalizer = 24.0 * rows_all
    projected = weighted / math.sqrt(normalizer)
    recip = 1.0 / (squares / normalizer + regularizer)
    row_ids = sp_pos * block_rows + lax.iota(jnp.int32, block_rows)
    col_ids = obs_pos * tile_cols + lax.iota(jnp.int32, tile_cols)
    all_ids = lax.iota(jnp.int32, sparse_count)
    on_diag = row_ids[:, None] == col_ids[None, :]
    reg_rows = lax.dynamic_slice_in_dim(regularizer, sp_pos * block_rows, block_rows)
    recip_rows = lax.dynamic_slice_in_dim(recip, sp_pos * block_rows, block_rows)
    recip_cols = lax.dynamic_slice_in_dim(recip, obs_pos * tile_cols, tile_cols)
    system_tile = gram_part.T / normalizer + jnp.where(on_diag, reg_rows[:, None], 0.0)
    highest = lax.Precision.HIGHEST
    system_full_rows = lax.all_gather(system_tile, "obs", axis=1, tiled=True)
    system_full_cols = lax.all_gather(system_tile, "sp", axis=0, tiled=True)
    first_rows = first_iterate(
        system_full_rows, recip_rows, recip, row_ids[:, None] == all_ids[None, :]
    )
    first_cols = first_iterate(
        system_full_cols, recip, recip_cols, all_ids[:, None] == col_ids[None, :]
    )
    product_tile = jnp.dot(system_full_rows, first_cols, precision=highest)
    product_full_cols = lax.all_gather(product_tile, "sp", axis=0, tiled=True)
    first_tile = first_iterate(system_tile, recip_rows, recip_cols, on_diag)
    inverse_tile = 2.0 * first_tile - jnp.dot(first_rows, product_full_cols, precision=highest)
    projected_cols = lax.dynamic_slice_in_dim(projected, obs_pos * tile_cols, tile_cols)
    weight_part = jnp.dot(inverse_tile, projected_cols, precision=highest)
    weights = lax.psum(weight_part, "obs")
    return (inverse_tile, weights)


def solution(mesh):
    in_specs = (P("obs", None), P("obs", None), P(), P("obs"), P())
    out_specs = (P("sp", "obs"), P("sp"))
    return jax.shard_map(
        on_device, mesh=mesh, in_specs=in_specs, out_specs=out_specs, check_vma=False
    )
```

profile of v0, /device:TPU:0, one launch (start us, length us, event | category | flops | bytes accessed | tf_op | source)
XLA Modules:
  0.0 955.4 jit_solution(15224427852561429307)
XLA Ops:
  7.2 0.7 fusion.36
  7.9 0.7 and_convert_fusion
  8.7 1.2 fusion.32
  9.9 1.2 fusion.33
  11.1 17.3 %gather_fusion = bf16[4096,512]{1,0:T(8,128)(2,1)} fusion(bf16[512,512]{1,0:T(8,128)(2,1)S(1)} %fusion.33, s32[4096]{0:T(1024)S(1)} %fusion.36), kind=kCustom, calls=%fused_computation | custom fusion | bytes 8404992 | tf_op jit(solution)/shard_map/gather | solution.py:29
  28.4 4.0 multiply_convert_fusion
  32.5 0.0 reduce-scatter.2.cloned.1.call-start
  32.6 1.1 copy-done.3
  33.7 0.3 fusion.22
  34.0 112.7 %all-reduce.3.cloned.1.call-done = bf16[4096,512]{1,0:T(8,128)(2,1)} async-done(((bf16[4096,512]{1,0:T(8,128)(2,1)}), bf16[4096,512]{1,0:T(8,128)(2,1)}) %all-reduce.3.cloned.1.call-update) | async-done | bytes 4194320 | tf_op jit(solution)/shard_map/psum | solution.py:52
  146.7 7.7 add_convert_fusion
  154.4 3.2 copy-done.2
  157.6 22.4 %fusion.17 = f32[4096,2048]{1,0:T(8,128)} fusion(bf16[1024,4096]{1,0:T(8,128)(2,1)S(1)} %add_convert_fusion, s32[]{:T(128)} %select_n.28), kind=kOutput, calls=%fused_computation.23 | convolution fusion | flops 17179869184 | bytes 46137348 | tf_op jit(solution)/shard_map/dot_general | solution.py:58
  180.1 0.0 all-gather.6.cloned.1.call-start
  180.2 331.8 %reduce-scatter.2.cloned.1.call-done = f32[256,2048]{1,0:T(8,128)} async-done(((f32[4096,2048]{1,0:T(8,128)}), f32[256,2048]{1,0:T(8,128)}) %reduce-scatter.2.cloned.1.call-update) | async-done | bytes 2097168 | tf_op jit(solution)/shard_map/reduce_scatter | solution.py:57
  512.0 3.3 fusion.26
  515.3 0.0 all-gather.4.cloned.1.call-start
  515.3 0.5 all-gather.4.cloned.1.call-update
  515.9 3.1 multiply_reduce_fusion
  519.0 3.3 fusion.15
  522.3 59.1 %all-reduce = (f32[2048]{0:T(1024)S(1)}, f32[2048]{0:T(1024)S(1)}) all-reduce(f32[2048]{0:T(1024)S(1)} %multiply_reduce_fusion, f32[2048]{0:T(1024)S(1)} %bitcast.13), channel_id=1, replica_groups=mesh['obs'=16,'sp'=2] {'obs'}, use_global_device_ids=true, to_apply=%region_4.5 | all-reduce | flops 4096 | bytes 32768 | tf_op jit(solution)/shard_map/psum | solution.py:67
  581.4 4.4 all_gather.15
  585.7 0.1 dynamic_slice.18
  585.8 155.6 %all-gather.4.cloned.1.call-done = f32[2048,4096]{0,1:T(8,128)} async-done(((f32[2048,256]{0,1:T(8,128)}), f32[2048,4096]{0,1:T(8,128)}) %all-gather.4.cloned.1.call-update) | async-done | bytes 33554448 | tf_op jit(solution)/shard_map/all_gather | solution.py:84
  741.4 67.7 %fusion.10 = f32[2048,256]{1,0:T(8,128)} fusion(f32[2048,4096]{0,1:T(8,128)} %all-gather.4.cloned.1.call-done, f32[4096,256]{0,1:T(8,128)} %all-gather.6.cloned.1.call-done, f32[256]{0:T(256)S(1)} %dynamic_slice.18, f32[4096]{0:T(1024)S(1)} %get-tuple-element.11, f32[4096]{0:T(1024)S(1)} %get-tuple-element.10, s32[256]{0:T(256)S(1)} %iota_add_fusion.1), kind=kOutput, calls=%fused_computation.15 | convolution fusion | flops 25775046656 | bytes 39880704 | tf_op jit(solution)/shard_map/dot_general | solution.py:92
  809.1 4.4 all_gather.19
  813.4 0.1 dynamic-slice_multiply_fusion
  813.5 52.5 %all-gather.8.cloned.1.call-done = f32[4096,256]{1,0:T(8,128)} async-done(((f32[2048,256]{1,0:T(8,128)}), f32[4096,256]{1,0:T(8,128)}) %all-gather.8.cloned.1.call-update) | async-done | bytes 4194320 | tf_op jit(solution)/shard_map/all_gather | solution.py:93
  866.0 44.1 %fusion.19 = f32[2048,256]{0,1:T(8,128)} fusion(f32[4096,256]{1,0:T(8,128)} %all-gather.8.cloned.1.call-done, f32[2048,4096]{0,1:T(8,128)} %all-gather.4.cloned.1.call-done, f32[4096]{0:T(1024)S(1)} %get-tuple-element.11, f32[2048]{0:T(1024)S(1)} %get-tuple-element.9, f32[2048]{0:T(1024)S(1)} %get-tuple-element.8, s32[2048]{0:T(1024)S(1)} %iota_add_fusion, ...), kind=kOutput, calls=%fused_computation.25 | convolution fusion | flops 25815416832 | bytes 41986048 | tf_op jit(solution)/shard_map/dot_general | solution.py:95
  910.1 3.0 copy.10
  913.1 1.2 fusion.41
  914.3 34.2 %psum.31 = f32[2048]{0:T(1024)} all-reduce(f32[2048]{0:T(1024)S(1)} %bitcast.12), channel_id=1, replica_groups=mesh['obs'=16,'sp'=2] {'obs'}, use_global_device_ids=true, to_apply=%region_7.8 | all-reduce | flops 2048 | bytes 16384 | tf_op jit(solution)/shard_map/psum | solution.py:98
  (26 shorter events, 0.2 us)
Async XLA Ops:
  7.2 139.6 %all-reduce.3.cloned.1.call-start = ((), (), s32[]{:S(2)}) async-start(), calls=%async_computation.1 | async-start | bytes 8388608 | tf_op jit(solution)/shard_map/psum | solution.py:52
  32.5 1.2 copy-start.3
  32.5 479.5 %reduce-scatter.2.cloned.1.call-start = ((), (), s32[]{:S(2)}) async-start(), calls=%async_computation.2 | async-start | bytes 35651584 | tf_op jit(solution)/shard_map/reduce_scatter | solution.py:57
  154.4 3.2 copy-start.2
  180.0 331.9 %dynamic-slice-start = ((f32[4096]{0:T(1024)}, s32[]{:T(128)}), f32[2048]{0:T(1024)S(1)}, s32[]{:S(2)}) async-start(f32[4096]{0:T(1024)} %param.9, s32[]{:T(128)} %select_n.28), calls=%async_computation.6 | async-start | bytes 16896 | tf_op jit(solution)/shard_map/dynamic_slice | solution.py:79
  180.1 405.7 %all-gather.6.cloned.1.call-start = ((), (), s32[]{:S(2)}) async-start(), calls=%async_computation.4 | async-start | bytes 6291456 | tf_op jit(solution)/shard_map/all_gather | solution.py:85
  180.1 335.8 %copy-start.5 = (bf16[1024]{0:T(1024)(128)(2,1)S(1)}, bf16[1024]{0:T(1024)(128)(2,1)}, u32[]{:S(2)}) copy-start(bf16[1024]{0:T(1024)(128)(2,1)} %param.8) | copy-start | bytes 6148
  515.3 226.1 %all-gather.4.cloned.1.call-start = ((), (), s32[]{:S(2)}) async-start(), calls=%async_computation.3 | async-start | bytes 35651584 | tf_op jit(solution)/shard_map/all_gather | solution.py:84
  515.9 350.1 %all-gather.8.cloned.1.call-start = ((), (), s32[]{:S(2)}) async-start(), calls=%async_computation.5 | async-start | bytes 6291456 | tf_op jit(solution)/shard_map/all_gather | solution.py:93
  515.9 69.8 %copy-start.4 = (f32[4096]{0:T(1024)S(1)}, f32[4096]{0:T(1024)}, u32[]{:S(2)}) copy-start(f32[4096]{0:T(1024)} %param.9) | copy-start | bytes 49156
  741.4 124.6 %copy-start = (f32[2048,256]{0,1:T(8,128)S(1)}, f32[2048,256]{0,1:T(8,128)}, u32[]{:S(2)}) copy-start(f32[2048,256]{0,1:T(8,128)} %fusion.26) | copy-start | bytes 6291460
  910.1 3.0 copy-start.1
Sparse Core Ops, SparseCore 0:
  32.6 114.0 all-reduce.2
  180.2 331.7 reduce-scatter.1
  515.4 55.7 all-gather.5
  573.3 168.0 all-gather.3
  809.2 56.7 all-gather.7
where the time goes:
time: 964 us; the launch traced here: 955 us
  waiting for transfers between devices  653 us (68%)
  matrix products  146 us (15%)
  blocking collectives  102 us (11%)
  local copies, waits for them, and re-layouts  24.8 us (3%)
  other arithmetic  14.6 us (2%)
  between operations  14.3 us (1%)
    reduce_scatter x1, waiting for transfers between devices, on_device(): lax.psum_scatter(lax.dot_general(full_kernel, own_kernel, (((0,), (0,)),...  332 us
    all_gather x1, waiting for transfers between devices, on_device(): system_full_rows = lax.all_gather(system_tile, 'obs', axis=1, tiled=True)  156 us
    psum x1, waiting for transfers between devices, on_device(): lax.psum(select_rows(candidate_units, sparse_index, cand_start).astype(jn...  113 us
    dot_general x1, matrix products, on_device(): product_tile = jnp.dot(system_full_rows, first_cols, precision=highest)  67.7 us
    psum x1, blocking collectives, on_device(): weighted, squares = lax.psum((weighted, squares), 'obs')  59.1 us
    all_gather x1, waiting for transfers between devices, on_device(): product_full_cols = lax.all_gather(product_tile, 'sp', axis=0, tiled=True)  52.5 us
    dot_general x1, matrix products, on_device(): jnp.dot(first_rows, product_full_cols, precision=highest)  44.1 us
    psum x1, blocking collectives, on_device(): weights = lax.psum(weight_part, 'obs')  34.2 us
  transfers between devices with their start and end apart: 5, of which 4 were waited for; matrix products, arithmetic and copies ran while one was open for 1% of the time, Pallas kernels for 0%

commit v1 on v0

--- a/solution.py
+++ b/solution.py
@@ -81,7 +81,18 @@
     recip_cols = lax.dynamic_slice_in_dim(recip, obs_pos * tile_cols, tile_cols)
     system_tile = gram_part.T / normalizer + jnp.where(on_diag, reg_rows[:, None], 0.0)
     highest = lax.Precision.HIGHEST
-    system_full_rows = lax.all_gather(system_tile, "obs", axis=1, tiled=True)
+    ways = lax.axis_size("obs")
+    up = [(d, (d + 1) % ways) for d in range(ways)]
+    down = [(d, (d - 1) % ways) for d in range(ways)]
+    earlier, later = ([system_tile], [system_tile])
+    for _ in range(ways // 2):
+        earlier.append(lax.ppermute(earlier[-1], "obs", up))
+    for _ in range((ways - 1) // 2):
+        later.append(lax.ppermute(later[-1], "obs", down))
+    line = jnp.concatenate([*earlier[::-1], *later[1:]], axis=1)
+    system_full_rows = jnp.roll(
+        line, (lax.axis_index("obs") - ways // 2) * system_tile.shape[1], axis=1
+    )
     system_full_cols = lax.all_gather(system_tile, "sp", axis=0, tiled=True)
     first_rows = first_iterate(
         system_full_rows, recip_rows, recip, row_ids[:, None] == all_ids[None, :]

time: 964 us -> 1180 us (1.22)
  starting transfers between devices: 0.2 us -> 228 us
  waiting for transfers between devices: 653 us -> 569 us
  local copies, waits for them, and re-layouts: 24.8 us -> 88.1 us
    ppermute x0 -> x15, starting transfers between devices: none -> 228 us  [the longest x8 223 us: on_device(): earlier.append(lax.ppermute(earlier[-1], 'obs', up))]
    all_gather x1 -> x0, waiting for transfers between devices: 156 us -> none  [on_device(): system_full_rows = lax.all_gather(system_tile, 'obs', axis=1, tiled=True)]
    ppermute x0 -> x15, waiting for transfers between devices: none -> 74.2 us  [the longest x8 74.2 us: on_device(): earlier.append(lax.ppermute(earlier[-1], 'obs', up))]
    unnamed x14 -> x85, local copies, waits for them, and re-layouts: 7.4 us -> 69.2 us
  transfers between devices with their start and end apart: 5 -> 19, of which waited for: 4 -> 10; matrix products, arithmetic and copies ran while one was open for 1% -> 6% of each run, Pallas kernels for 0% -> 0%
where the time goes in v1:
time: 1180 us; the launch traced here: 1170 us
  waiting for transfers between devices  569 us (48%)
  starting transfers between devices  228 us (19%)
  matrix products  138 us (12%)
  blocking collectives  113 us (10%)
  local copies, waits for them, and re-layouts  88.1 us (7%)
  other arithmetic  16.8 us (1%)
  between operations  14.2 us (1%)
    reduce_scatter x1, waiting for transfers between devices, on_device(): lax.psum_scatter(lax.dot_general(full_kernel, own_kernel, (((0,), (0,)),...  331 us
    ppermute x8, starting transfers between devices, on_device(): earlier.append(lax.ppermute(earlier[-1], 'obs', up))  223 us
    psum x1, waiting for transfers between devices, on_device(): lax.psum(select_rows(candidate_units, sparse_index, cand_start).astype(jn...  114 us
    ppermute x8, waiting for transfers between devices, on_device(): earlier.append(lax.ppermute(earlier[-1], 'obs', up))  74.2 us
    psum x1, blocking collectives, on_device(): weighted, squares = lax.psum((weighted, squares), 'obs')  70 us
    unnamed x85, local copies, waits for them, and re-layouts  69.2 us
    dot_general x1, matrix products, on_device(): product_tile = jnp.dot(system_full_rows, first_cols, precision=highest)  58.7 us
    all_gather x1, waiting for transfers between devices, on_device(): product_full_cols = lax.all_gather(product_tile, 'sp', axis=0, tiled=True)  49.7 us
  transfers between devices with their start and end apart: 19, of which 10 were waited for; matrix products, arithmetic and copies ran while one was open for 6% of the time, Pallas kernels for 0%

profile of v1, /device:TPU:0, one launch (start us, length us, event | category | flops | bytes accessed | tf_op | source)
XLA Modules:
  0.0 1167.9 jit_solution(7261270081943939982)
XLA Ops:
  11.1 17.4 %gather_fusion = bf16[4096,512]{1,0:T(8,128)(2,1)} fusion(bf16[512,512]{1,0:T(8,128)(2,1)S(1)} %fusion.35, s32[4096]{0:T(1024)S(1)} %fusion.38), kind=kCustom, calls=%fused_computation | custom fusion | bytes 8404992 | tf_op jit(solution)/shard_map/gather | solution.py:29
  28.5 4.2 multiply_convert_fusion
  33.0 113.9 %all-reduce.3.cloned.1.call-done = bf16[4096,512]{1,0:T(8,128)(2,1)} async-done(((bf16[4096,512]{1,0:T(8,128)(2,1)}), bf16[4096,512]{1,0:T(8,128)(2,1)}) %all-reduce.3.cloned.1.call-update) | async-done | bytes 4194320 | tf_op jit(solution)/shard_map/psum | solution.py:52
  146.9 7.7 add_convert_fusion
  154.6 3.2 copy-done.23
  157.9 22.4 %fusion.19 = f32[4096,2048]{1,0:T(8,128)} fusion(bf16[1024,4096]{1,0:T(8,128)(2,1)S(1)} %add_convert_fusion, s32[]{:T(128)S(6)} %select_n.41), kind=kOutput, calls=%fused_computation.25 | convolution fusion | flops 17179869184 | bytes 46137348 | tf_op jit(solution)/shard_map/dot_general | solution.py:58
  181.0 331.2 %reduce-scatter.2.cloned.1.call-done = f32[256,2048]{1,0:T(8,128)} async-done(((f32[4096,2048]{1,0:T(8,128)}), f32[256,2048]{1,0:T(8,128)}) %reduce-scatter.2.cloned.1.call-update) | async-done | bytes 2097168 | tf_op jit(solution)/shard_map/reduce_scatter | solution.py:57
  514.2 28.1 %collective-permute-done = f32[2048,256]{0,1:T(8,128)S(1)} collective-permute-done((f32[2048,256]{0,1:T(8,128)S(1)}, f32[2048,256]{0,1:T(8,128)S(1)}, u32[]{:S(2)}, u32[]{:S(2)}) %collective-permute-start) | collective-permute-done | bytes 2097184 | tf_op jit(solution)/shard_map/ppermute | solution.py:89
  542.4 4.4 collective-permute-start.8
  546.8 23.8 %collective-permute-done.1 = f32[2048,256]{0,1:T(8,128)S(1)} collective-permute-done((f32[2048,256]{0,1:T(8,128)S(1)}, f32[2048,256]{0,1:T(8,128)S(1)}, u32[]{:S(2)}, u32[]{:S(2)}) %collective-permute-start.1) | collective-permute-done | bytes 2097184 | tf_op jit(solution)/shard_map/ppermute | solution.py:89
  570.6 16.1 %collective-permute-start.2 = (f32[2048,256]{0,1:T(8,128)S(1)}, f32[2048,256]{0,1:T(8,128)S(1)}, u32[]{:S(2)}, u32[]{:S(2)}) collective-permute-start(f32[2048,256]{0,1:T(8,128)S(1)} %collective-permute-done.1), channel_id=1, source_target_pairs={{0,2},{2,4},{4,6},{6,8},{8,10},{10,12},{12,14},{14,16},{16,18},{18... | collective-permute-start | bytes 6291464 | tf_op jit(solution)/shard_map/ppermute | solution.py:89
  588.1 10.8 collective-permute-done.2
  598.9 33.4 %collective-permute-start.3 = (f32[2048,256]{0,1:T(8,128)S(1)}, f32[2048,256]{0,1:T(8,128)S(1)}, u32[]{:S(2)}, u32[]{:S(2)}) collective-permute-start(f32[2048,256]{0,1:T(8,128)S(1)} %collective-permute-done.2), channel_id=1, source_target_pairs={{0,2},{2,4},{4,6},{6,8},{8,10},{10,12},{12,14},{14,16},{16,18},{18... | collective-permute-start | bytes 6291464 | tf_op jit(solution)/shard_map/ppermute | solution.py:89
  636.3 43.4 %collective-permute-start.4 = (f32[2048,256]{0,1:T(8,128)S(1)}, f32[2048,256]{0,1:T(8,128)S(1)}, u32[]{:S(2)}, u32[]{:S(2)}) collective-permute-start(f32[2048,256]{0,1:T(8,128)S(1)} %collective-permute-done.3), channel_id=1, source_target_pairs={{0,2},{2,4},{4,6},{6,8},{8,10},{10,12},{12,14},{14,16},{16,18},{18... | collective-permute-start | bytes 6291464 | tf_op jit(solution)/shard_map/ppermute | solution.py:89
  683.5 42.7 %collective-permute-start.5 = (f32[2048,256]{0,1:T(8,128)S(1)}, f32[2048,256]{0,1:T(8,128)S(1)}, u32[]{:S(2)}, u32[]{:S(2)}) collective-permute-start(f32[2048,256]{0,1:T(8,128)S(1)} %collective-permute-done.4), channel_id=1, source_target_pairs={{0,2},{2,4},{4,6},{6,8},{8,10},{10,12},{12,14},{14,16},{16,18},{18... | collective-permute-start | bytes 6291464 | tf_op jit(solution)/shard_map/ppermute | solution.py:89
  730.0 44.1 %collective-permute-start.6 = (f32[2048,256]{0,1:T(8,128)S(1)}, f32[2048,256]{0,1:T(8,128)}, u32[]{:S(2)}, u32[]{:S(2)}) collective-permute-start(f32[2048,256]{0,1:T(8,128)S(1)} %collective-permute-done.5), channel_id=1, source_target_pairs={{0,2},{2,4},{4,6},{6,8},{8,10},{10,12},{12,14},{14,16},{16,18},{18... | collective-permute-start | bytes 6291464 | tf_op jit(solution)/shard_map/ppermute | solution.py:89
  774.2 3.9 collective-permute-done.6
  778.1 43.6 %collective-permute-start.7 = (f32[2048,256]{0,1:T(8,128)}, f32[2048,256]{0,1:T(8,128)}, u32[]{:S(2)}, u32[]{:S(2)}) collective-permute-start(f32[2048,256]{0,1:T(8,128)} %collective-permute-done.6), channel_id=1, source_target_pairs={{0,2},{2,4},{4,6},{6,8},{8,10},{10,12},{12,14},{14,16},{16,18},{18... | collective-permute-start | bytes 6291464 | tf_op jit(solution)/shard_map/ppermute | solution.py:89
  827.6 70.0 %all-reduce = (f32[2048]{0:T(1024)S(1)}, f32[2048]{0:T(1024)S(1)}) all-reduce(f32[2048]{0:T(1024)S(1)} %multiply_reduce_fusion, f32[2048]{0:T(1024)S(1)} %bitcast.16), channel_id=1, replica_groups=mesh['obs'=16,'sp'=2] {'obs'}, use_global_device_ids=true, to_apply=%region_4.5 | all-reduce | flops 4096 | bytes 32768 | tf_op jit(solution)/shard_map/psum | solution.py:67
  897.6 4.4 all_gather.12
  902.2 3.3 constant_dynamic-update-slice_fusion.31
  905.5 3.6 constant_dynamic-update-slice_fusion.30
  925.9 3.2 constant_dynamic-update-slice_fusion.18
  929.1 3.1 constant_dynamic-update-slice_fusion.17
  936.8 3.1 constant_dynamic-update-slice_fusion.14
  956.5 3.1 constant_dynamic-update-slice_fusion.2
  959.6 3.2 constant_dynamic-update-slice_fusion.1
  964.3 58.7 %fusion.5 = f32[2048,256]{1,0:T(8,128)} fusion(f32[2048,8192]{0,1:T(8,128)} %constant_dynamic-update-slice_fusion, s32[]{:T(128)S(6)} %select_n.47, f32[4096,256]{0,1:T(8,128)} %all-gather.3.cloned.1.call-done, f32[256]{0:T(256)S(1)} %dynamic_slice.22, f32[4096]{0:T(1024)S(1)} %get-tuple-element.11, f32[4096]{0:T(1024)S(1)} %get-tuple-element.10, ...), kind=kOutput, calls=%fused_computation.7 | convolution fusion | flops 25775046656 | bytes 39880708 | tf_op jit(solution)/shard_map/dot_general | solution.py:103
  1023.0 4.4 all_gather.15
  1027.4 49.7 %all-gather.5.cloned.1.call-done = f32[4096,256]{1,0:T(8,128)} async-done(((f32[2048,256]{1,0:T(8,128)}), f32[4096,256]{1,0:T(8,128)}) %all-gather.5.cloned.1.call-update) | async-done | bytes 4194320 | tf_op jit(solution)/shard_map/all_gather | solution.py:104
  1077.1 44.1 %fusion.21 = f32[2048,256]{0,1:T(8,128)} fusion(f32[4096,256]{1,0:T(8,128)} %all-gather.5.cloned.1.call-done, f32[2048,8192]{0,1:T(8,128)} %constant_dynamic-update-slice_fusion, s32[]{:T(128)S(6)} %select_n.47, f32[4096]{0:T(1024)S(1)} %get-tuple-element.11, f32[2048]{0:T(1024)S(1)} %get-tuple-element.9, f32[2048]{0:T(1024)S(1)} %get-tuple-element.8, ...), kind=kOutput, calls=%fused_computation.27 | convolution fusion | flops 25815416832 | bytes 42010628 | tf_op jit(solution)/shard_map/dot_general | solution.py:106
  1126.8 34.3 %psum.31 = f32[2048]{0:T(1024)} all-reduce(f32[2048]{0:T(1024)S(1)} %bitcast.15), channel_id=1, replica_groups=mesh['obs'=16,'sp'=2] {'obs'}, use_global_device_ids=true, to_apply=%region_7.8 | all-reduce | flops 2048 | bytes 16384 | tf_op jit(solution)/shard_map/psum | solution.py:109
  (126 shorter events, 71.1 us)
Async XLA Ops:
  7.2 139.8 %all-reduce.3.cloned.1.call-start = ((), (), s32[]{:S(2)}) async-start(), calls=%async_computation.1 | async-start | bytes 8388608 | tf_op jit(solution)/shard_map/psum | solution.py:52
  32.7 479.5 %reduce-scatter.2.cloned.1.call-start = ((), (), s32[]{:S(2)}) async-start(), calls=%async_computation.2 | async-start | bytes 35651584 | tf_op jit(solution)/shard_map/reduce_scatter | solution.py:57
  180.3 641.4 %copy-start.26 = (bf16[1024]{0:T(1024)(128)(2,1)S(1)}, bf16[1024]{0:T(1024)(128)(2,1)}, u32[]{:S(2)}) copy-start(bf16[1024]{0:T(1024)(128)(2,1)} %param.8) | copy-start | bytes 6148
  180.3 783.9 %all-gather.3.cloned.1.call-start = ((), (), s32[]{:S(2)}) async-start(), calls=%async_computation.3 | async-start | bytes 6291456 | tf_op jit(solution)/shard_map/all_gather | solution.py:96
  514.1 387.9 %copy-start.1 = (f32[2048,256]{0,1:T(8,128)}, f32[2048,256]{0,1:T(8,128)S(1)}, u32[]{:S(2)}) copy-start(f32[2048,256]{0,1:T(8,128)S(1)} %fusion.28) | copy-start | bytes 6291460
  514.1 28.2 %collective-permute-start = (f32[2048,256]{0,1:T(8,128)S(1)}, f32[2048,256]{0,1:T(8,128)S(1)}, u32[]{:S(2)}, u32[]{:S(2)}) collective-permute-start(f32[2048,256]{0,1:T(8,128)S(1)} %fusion.28), channel_id=1, source_target_pairs={{0,2},{2,4},{4,6},{6,8},{8,10},{10,12},{12,14},{14,16},{16,18},{18... | collective-permute-start | bytes 6291464 | tf_op jit(solution)/shard_map/ppermute | solution.py:89
  542.4 44.4 %copy-start.3 = (f32[2048,256]{0,1:T(8,128)}, f32[2048,256]{0,1:T(8,128)S(1)}, u32[]{:S(2)}) copy-start(f32[2048,256]{0,1:T(8,128)S(1)} %collective-permute-done) | copy-start | bytes 6291460
  542.4 28.3 %collective-permute-start.1 = (f32[2048,256]{0,1:T(8,128)S(1)}, f32[2048,256]{0,1:T(8,128)S(1)}, u32[]{:S(2)}, u32[]{:S(2)}) collective-permute-start(f32[2048,256]{0,1:T(8,128)S(1)} %collective-permute-done), channel_id=1, source_target_pairs={{0,2},{2,4},{4,6},{6,8},{8,10},{10,12},{12,14},{14,16},{16,18},{18... | collective-permute-start | bytes 6291464 | tf_op jit(solution)/shard_map/ppermute | solution.py:89
  542.4 44.4 %collective-permute-start.8 = (f32[2048,256]{0,1:T(8,128)S(1)}, f32[2048,256]{0,1:T(8,128)S(1)}, u32[]{:S(2)}, u32[]{:S(2)}) collective-permute-start(f32[2048,256]{0,1:T(8,128)S(1)} %fusion.28), channel_id=1, source_target_pairs={{0,30},{2,0},{4,2},{6,4},{8,6},{10,8},{12,10},{14,12},{16,14},{18,... | collective-permute-start | bytes 6291464 | tf_op jit(solution)/shard_map/ppermute | solution.py:91
  570.6 61.7 %copy-start.7 = (f32[2048,256]{0,1:T(8,128)}, f32[2048,256]{0,1:T(8,128)S(1)}, u32[]{:S(2)}) copy-start(f32[2048,256]{0,1:T(8,128)S(1)} %collective-permute-done.1) | copy-start | bytes 6291460
  570.6 28.3 %collective-permute-start.2 = (f32[2048,256]{0,1:T(8,128)S(1)}, f32[2048,256]{0,1:T(8,128)S(1)}, u32[]{:S(2)}, u32[]{:S(2)}) collective-permute-start(f32[2048,256]{0,1:T(8,128)S(1)} %collective-permute-done.1), channel_id=1, source_target_pairs={{0,2},{2,4},{4,6},{6,8},{8,10},{10,12},{12,14},{14,16},{16,18},{18... | collective-permute-start | bytes 6291464 | tf_op jit(solution)/shard_map/ppermute | solution.py:89
  586.8 45.5 %collective-permute-start.9 = (f32[2048,256]{0,1:T(8,128)S(1)}, f32[2048,256]{0,1:T(8,128)S(1)}, u32[]{:S(2)}, u32[]{:S(2)}) collective-permute-start(f32[2048,256]{0,1:T(8,128)S(1)} %collective-permute-done.8), channel_id=1, source_target_pairs={{0,30},{2,0},{4,2},{6,4},{8,6},{10,8},{12,10},{14,12},{16,14},{18,... | collective-permute-start | bytes 6291464 | tf_op jit(solution)/shard_map/ppermute | solution.py:91
  598.9 80.8 %copy-start.11 = (f32[2048,256]{0,1:T(8,128)}, f32[2048,256]{0,1:T(8,128)S(1)}, u32[]{:S(2)}) copy-start(f32[2048,256]{0,1:T(8,128)S(1)} %collective-permute-done.2) | copy-start | bytes 6291460
  598.9 37.4 %collective-permute-start.3 = (f32[2048,256]{0,1:T(8,128)S(1)}, f32[2048,256]{0,1:T(8,128)S(1)}, u32[]{:S(2)}, u32[]{:S(2)}) collective-permute-start(f32[2048,256]{0,1:T(8,128)S(1)} %collective-permute-done.2), channel_id=1, source_target_pairs={{0,2},{2,4},{4,6},{6,8},{8,10},{10,12},{12,14},{14,16},{16,18},{18... | collective-permute-start | bytes 6291464 | tf_op jit(solution)/shard_map/ppermute | solution.py:89
  632.3 47.4 %collective-permute-start.10 = (f32[2048,256]{0,1:T(8,128)S(1)}, f32[2048,256]{0,1:T(8,128)S(1)}, u32[]{:S(2)}, u32[]{:S(2)}) collective-permute-start(f32[2048,256]{0,1:T(8,128)S(1)} %collective-permute-done.9), channel_id=1, source_target_pairs={{0,30},{2,0},{4,2},{6,4},{8,6},{10,8},{12,10},{14,12},{16,14},{18,... | collective-permute-start | bytes 6291464 | tf_op jit(solution)/shard_map/ppermute | solution.py:91
  636.3 137.9 %copy-start.17 = (f32[2048,256]{0,1:T(8,128)}, f32[2048,256]{0,1:T(8,128)S(1)}, u32[]{:S(2)}) copy-start(f32[2048,256]{0,1:T(8,128)S(1)} %collective-permute-done.3) | copy-start | bytes 6291460
  636.3 47.2 %collective-permute-start.4 = (f32[2048,256]{0,1:T(8,128)S(1)}, f32[2048,256]{0,1:T(8,128)S(1)}, u32[]{:S(2)}, u32[]{:S(2)}) collective-permute-start(f32[2048,256]{0,1:T(8,128)S(1)} %collective-permute-done.3), channel_id=1, source_target_pairs={{0,2},{2,4},{4,6},{6,8},{8,10},{10,12},{12,14},{14,16},{16,18},{18... | collective-permute-start | bytes 6291464 | tf_op jit(solution)/shard_map/ppermute | solution.py:89
  679.7 46.5 %collective-permute-start.11 = (f32[2048,256]{0,1:T(8,128)S(1)}, f32[2048,256]{0,1:T(8,128)S(1)}, u32[]{:S(2)}, u32[]{:S(2)}) collective-permute-start(f32[2048,256]{0,1:T(8,128)S(1)} %collective-permute-done.10), channel_id=1, source_target_pairs={{0,30},{2,0},{4,2},{6,4},{8,6},{10,8},{12,10},{14,12},{16,14},{18,... | collective-permute-start | bytes 6291464 | tf_op jit(solution)/shard_map/ppermute | solution.py:91
  683.5 90.7 %copy-start.19 = (f32[2048,256]{0,1:T(8,128)}, f32[2048,256]{0,1:T(8,128)S(1)}, u32[]{:S(2)}) copy-start(f32[2048,256]{0,1:T(8,128)S(1)} %collective-permute-done.4) | copy-start | bytes 6291460
  683.5 46.5 %collective-permute-start.5 = (f32[2048,256]{0,1:T(8,128)S(1)}, f32[2048,256]{0,1:T(8,128)S(1)}, u32[]{:S(2)}, u32[]{:S(2)}) collective-permute-start(f32[2048,256]{0,1:T(8,128)S(1)} %collective-permute-done.4), channel_id=1, source_target_pairs={{0,2},{2,4},{4,6},{6,8},{8,10},{10,12},{12,14},{14,16},{16,18},{18... | collective-permute-start | bytes 6291464 | tf_op jit(solution)/shard_map/ppermute | solution.py:89
  727.5 46.6 %collective-permute-start.12 = (f32[2048,256]{0,1:T(8,128)S(1)}, f32[2048,256]{0,1:T(8,128)}, u32[]{:S(2)}, u32[]{:S(2)}) collective-permute-start(f32[2048,256]{0,1:T(8,128)S(1)} %collective-permute-done.11), channel_id=1, source_target_pairs={{0,30},{2,0},{4,2},{6,4},{8,6},{10,8},{12,10},{14,12},{16,14},{18,... | collective-permute-start | bytes 6291464 | tf_op jit(solution)/shard_map/ppermute | solution.py:91
  730.0 48.1 %copy-start.21 = (f32[2048,256]{0,1:T(8,128)}, f32[2048,256]{0,1:T(8,128)S(1)}, u32[]{:S(2)}) copy-start(f32[2048,256]{0,1:T(8,128)S(1)} %collective-permute-done.5) | copy-start | bytes 6291460
  730.0 48.1 %collective-permute-start.6 = (f32[2048,256]{0,1:T(8,128)S(1)}, f32[2048,256]{0,1:T(8,128)}, u32[]{:S(2)}, u32[]{:S(2)}) collective-permute-start(f32[2048,256]{0,1:T(8,128)S(1)} %collective-permute-done.5), channel_id=1, source_target_pairs={{0,2},{2,4},{4,6},{6,8},{8,10},{10,12},{12,14},{14,16},{16,18},{18... | collective-permute-start | bytes 6291464 | tf_op jit(solution)/shard_map/ppermute | solution.py:89
  774.2 128.0 %collective-permute-start.13 = (f32[2048,256]{0,1:T(8,128)}, f32[2048,256]{0,1:T(8,128)}, u32[]{:S(2)}, u32[]{:S(2)}) collective-permute-start(f32[2048,256]{0,1:T(8,128)} %collective-permute-done.12), channel_id=1, source_target_pairs={{0,30},{2,0},{4,2},{6,4},{8,6},{10,8},{12,10},{14,12},{16,14},{18,... | collective-permute-start | bytes 6291464 | tf_op jit(solution)/shard_map/ppermute | solution.py:91
  778.1 124.1 %collective-permute-start.7 = (f32[2048,256]{0,1:T(8,128)}, f32[2048,256]{0,1:T(8,128)}, u32[]{:S(2)}, u32[]{:S(2)}) collective-permute-start(f32[2048,256]{0,1:T(8,128)} %collective-permute-done.6), channel_id=1, source_target_pairs={{0,2},{2,4},{4,6},{6,8},{8,10},{10,12},{12,14},{14,16},{16,18},{18... | collective-permute-start | bytes 6291464 | tf_op jit(solution)/shard_map/ppermute | solution.py:89
  902.0 10.1 copy-start.18
  902.0 175.1 %all-gather.5.cloned.1.call-start = ((), (), s32[]{:S(2)}) async-start(), calls=%async_computation.4 | async-start | bytes 6291456 | tf_op jit(solution)/shard_map/all_gather | solution.py:104
  902.1 7.0 copy-start.22
  902.1 8.5 copy-start.20
  902.1 30.1 %collective-permute-start.14 = (f32[2048,256]{0,1:T(8,128)}, f32[2048,256]{0,1:T(8,128)S(1)}, u32[]{:S(2)}, u32[]{:S(2)}) collective-permute-start(f32[2048,256]{0,1:T(8,128)} %collective-permute-done.13), channel_id=1, source_target_pairs={{0,30},{2,0},{4,2},{6,4},{8,6},{10,8},{12,10},{14,12},{16,14},{18,... | collective-permute-start | bytes 6291464 | tf_op jit(solution)/shard_map/ppermute | solution.py:91
  905.5 8.2 copy-start.12
  964.3 112.9 %copy-start.2 = (f32[2048,256]{0,1:T(8,128)S(1)}, f32[2048,256]{0,1:T(8,128)}, u32[]{:S(2)}) copy-start(f32[2048,256]{0,1:T(8,128)} %copy-done.1) | copy-start | bytes 6291460
  (14 other events, 56.3 us)
Sparse Core Ops, SparseCore 0:
  32.8 114.0 all-reduce.2
  180.4 331.6 reduce-scatter.1
  902.2 53.9 all-gather.2
  1023.1 53.9 all-gather.4
